TPU v7x, 128 devices: a whole 4x4x4 slice. The times are simulated.
128 devices in a mesh: dp: 4 (over x_lo, core), ctx: 32 (over x_hi, y, z).
Axes of the slice: x: 4 (x_hi: 2, x_lo: 2; x = x_hi * 2 + x_lo), y: 4, z: 4, core: 2. Of those that a mesh axis runs over, the one named last changes fastest.
Arguments:
- frames: bfloat16 [4, 160, 16, 16, 512], P('dp', 'ctx'), may hold values from -6 to 6
- stream: bfloat16 [4, 160, 64, 3072], P('dp', 'ctx'), may hold values from -6 to 6
- video_frames: int32 [4], P('dp'), may hold values from 1 to 160
- conv_weight: bfloat16 [3, 3, 3, 512, 512], replicated, may hold values from -0.0546875 to 0.0546875
- latent_weight: bfloat16 [512, 16], replicated, may hold values from -0.25 to 0.25
- embed_weight: bfloat16 [64, 3072], replicated, may hold values from -0.75 to 0.75
- norm_gain: float32 [3072], replicated, may hold values from 0.25 to 1.75
- qkv_weight: bfloat16 [3072, 4608], P('ctx', 'dp'), may hold values from -0.109375 to 0.109375
Outputs:
- section: bfloat16 [4, 160, 16, 16, 512], P('dp', 'ctx')
- mixed: bfloat16 [4, 160, 64, 1536], P('dp', 'ctx')
All inputs are finite; a program needn't handle non-finite values.
Results may differ from a plain program's by a relative error of at most 0.0061.
Values may be sent and summed in bfloat16 or wider, within the bound.
A program may use at most 128 MiB of HBM per device.

v0:
```python
import jax
import jax.numpy as jnp
from jax import lax
from jax.sharding import Mesh
from jax.sharding import PartitionSpec as P

HD = 128
CTX = ("ctx_0", "ctx_1", "ctx_2")


def passed_along(value, axis, steps):
    count = lax.axis_size(axis)
    leading, last = (max(0, -steps), min(count, count - steps))
    return lax.ppermute(value, axis, [(source, source + steps) for source in range(leading, last)])


def from_everyone(array, axis):
    length = lax.axis_size(axis)
    return lax.all_to_all(
        jnp.broadcast_to(array[None], (length, *array.shape)), axis, 0, 0, tiled=True
    )


def laid_out(tiles, dim):
    dims = list(tiles.shape[1:])
    dims[dim] *= tiles.shape[0]
    return jnp.moveaxis(tiles, 0, dim).reshape(dims)


def gathered_copies(array, axis, dim):
    tiles = from_everyone(array, axis)
    return laid_out(tiles, dim)


def all_blocks(array, axes, turns):
    tiles = array[None]
    for k in turns:
        tiles = lax.all_gather(tiles, axes[k], axis=0, tiled=True)
    current = [lax.axis_size(axes[k]) for k in reversed(turns)]
    tiles = tiles.reshape(*current, *array.shape)
    turned = sorted(range(len(turns)), key=lambda place: turns[len(turns) - 1 - place])
    return tiles.transpose(*turned, *range(len(turns), tiles.ndim)).reshape(-1, *array.shape)


def gather_axes(array, axes, turns, dim):
    return laid_out(all_blocks(array, axes, turns), dim)


def attend(lengths, block):
    head_size = block.shape[-1] // 3
    slots = block.shape[1]
    query = block[..., 0:head_size]
    keys = block[..., head_size : 2 * head_size]
    values = block[..., 2 * head_size : 3 * head_size]
    scores = jnp.einsum(
        "gtphd,gsphd->gphts", query, keys, preferred_element_type=jnp.float32
    ) * head_size ** (-0.5)
    frame_ids = jnp.arange(slots, dtype=jnp.int32)
    video = frame_ids[None, :] < lengths[:, None]
    allowed = (
        video[:, :, None] & video[:, None, :] | (frame_ids[:, None] == frame_ids[None, :])[None]
    )
    scores = jnp.where(allowed[:, None, None], scores, -1e30)
    top = jnp.max(scores, axis=-1, keepdims=True)
    expo = jnp.exp(scores - top)
    probs = (expo / jnp.sum(expo, axis=-1, keepdims=True)).astype(jnp.bfloat16)
    out = jnp.einsum(
        "gphts,gsphd->gtphd", probs, values, preferred_element_type=jnp.float32
    ).astype(jnp.bfloat16)
    return lax.all_to_all(out, CTX, split_axis=1, concat_axis=2, tiled=True)


def on_device(
    frames, stream, video_frames, conv_weight, latent_weight, embed_weight, norm_gain, qkv_weight
):
    f_dev, height, width, channels = (
        frames.shape[1],
        frames.shape[2],
        frames.shape[3],
        frames.shape[4],
    )
    width_model = stream.shape[3]
    tokens_frame = stream.shape[2]
    act = jax.nn.silu(frames.astype(jnp.float32)).astype(jnp.bfloat16)
    past = passed_along(act[:, f_dev - 2 :], CTX, 1)
    joined = jnp.concatenate([past, act], axis=1)[0]
    padded = jnp.pad(joined, ((0, 0), (1, 1), (1, 1), (0, 0)))
    length = video_frames[0]
    frame_ids = lax.axis_index(CTX) * f_dev + jnp.arange(f_dev, dtype=jnp.int32)
    cells = f_dev * height * width
    total = jnp.zeros((cells, channels), jnp.float32)
    for lag in range(3):
        part = jnp.zeros((cells, channels), jnp.float32)
        for row in range(3):
            for col in range(3):
                slab = padded[
                    2 - lag : 2 - lag + f_dev, row : row + height, col : col + width, :
                ].reshape(-1, channels)
                part = part + jnp.dot(
                    slab, conv_weight[lag, row, col], preferred_element_type=jnp.float32
                )
        if lag == 0:
            total = part
        else:
            valid = ((frame_ids < length) & (frame_ids >= lag)).astype(jnp.float32)
            total = total + part * jnp.repeat(valid, height * width)[:, None]
    section = (frames.astype(jnp.float32) + total.reshape(frames.shape)).astype(jnp.bfloat16)
    latent = jnp.dot(
        section.reshape(-1, channels), latent_weight, preferred_element_type=jnp.float32
    ).astype(jnp.bfloat16)
    lat_size = latent.shape[1]
    latent = latent.reshape(f_dev, height // 2, 2, width // 2, 2, lat_size).transpose(
        0, 1, 3, 2, 4, 5
    )
    patches = latent.reshape(-1, 4 * lat_size)
    embedded = jnp.dot(patches, embed_weight, preferred_element_type=jnp.float32) + stream.reshape(
        -1, width_model
    ).astype(jnp.float32)
    scale = lax.rsqrt(jnp.mean(embedded * embedded, axis=-1, keepdims=True) + 1e-06)
    normed = (embedded * scale * norm_gain).astype(jnp.bfloat16)
    head_size = HD
    gathered, lengths = (
        gathered_copies(normed.reshape(1, -1, width_model), "dp", 0),
        gathered_copies(video_frames, "dp", 0),
    )
    group_count = gathered.shape[0]
    all_rows = gathered.reshape(-1, width_model)
    qkv = jnp.dot(
        all_rows, gather_axes(qkv_weight, CTX, (0, 1, 2), 0), preferred_element_type=jnp.float32
    )
    qkv = qkv.astype(jnp.bfloat16).reshape(
        group_count, f_dev, tokens_frame, qkv_weight.shape[1] // (3 * head_size), 3 * head_size
    )
    mixed = attend(lengths, lax.all_to_all(qkv, CTX, split_axis=2, concat_axis=1, tiled=True))
    mixed = lax.all_to_all(mixed, "dp", split_axis=0, concat_axis=3, tiled=True)
    return (section, mixed.reshape(1, f_dev, tokens_frame, -1))


def solution(mesh):
    finer = Mesh(mesh.devices.reshape(mesh.shape["dp"], 2, 4, 4), ("dp", "ctx_0", "ctx_1", "ctx_2"))
    return jax.shard_map(
        on_device,
        mesh=finer,
        in_specs=(
            P("dp", CTX, None, None, None),
            P("dp", CTX, None, None),
            P("dp"),
            P(),
            P(),
            P(),
            P(),
            P(CTX, "dp"),
        ),
        out_specs=(P("dp", CTX, None, None, None), P("dp", CTX, None, None)),
        check_vma=False,
    )
```

profile of v0, /device:TPU:1, one launch (start us, length us, event | category | flops | bytes accessed | tf_op | source)
XLA Modules:
  0.0 339.0 jit_solution(1459822168728964891)
XLA Ops:
  7.2 2.2 fusion.9
  9.5 4.4 %collective-permute-start = (bf16[1,2,16,16,512]{4,3,2,1,0:T(8,128)(2,1)S(1)}, bf16[1,2,16,16,512]{4,3,2,1,0:T(8,128)(2,1)S(1)}, u32[]{:S(2)}, u32[]{:S(2)}) collective-permute-start(bf16[1,2,16,16,512]{4,3,2,1,0:T(8,128)(2,1)S(1)} %slice.235), channel_id=1, source_target_pairs={{0,1},{1,2},{2,3},{3,4},{4,5},{5,6},{6,7},{7,8},{8,9},{9,10},{10,1... | collective-permute-start | bytes 1572872 | tf_op jit(solution)/shard_map/ppermute | solution.py:14
  13.9 8.3 %all-gather = bf16[192,1152]{1,0:T(8,128)(2,1)} all-gather(bf16[96,1152]{1,0:T(8,128)(2,1)S(1)} %copy-done.28), channel_id=2, replica_groups=mesh['dp'=4,'ctx_0'=2,'ctx_1'=4,'ctx_2'=4] {'ctx_0'}, dimensions={0}, use_global_device_ids=true | all-gather | bytes 663552 | tf_op jit(solution)/shard_map/all_gather | solution.py:38
  23.1 1.3 collective-permute-done
  24.6 11.2 %pad_slice_fusion = (bf16[5,16,16,512]{3,2,1,0:T(8,128)(2,1)}, bf16[5,16,16,512]{3,2,1,0:T(8,128)(2,1)}, bf16[5,16,16,512]{3,2,1,0:T(8,128)(2,1)}, bf16[5,16,16,...) fusion(bf16[7,16,16,512]{3,2,1,0:T(8,128)(2,1)S(1)} %fusion.15), kind=kLoop, calls=%fused_computation.1 | loop fusion | bytes 26738688 | tf_op jit(solution)/shard_map/slice | solution.py:96
  35.8 3.8 %pad_slice_fusion.1 = (bf16[5,16,16,512]{3,2,1,0:T(8,128)(2,1)}, bf16[5,16,16,512]{3,2,1,0:T(8,128)(2,1)}, bf16[5,16,16,512]{3,2,1,0:T(8,128)(2,1)}, bf16[5,16,1...) fusion(bf16[7,16,16,512]{3,2,1,0:T(8,128)(2,1)S(1)} %fusion.15), kind=kLoop, calls=%fused_computation.2 | loop fusion | bytes 8388608 | tf_op jit(solution)/shard_map/slice | solution.py:96
  41.9 0.9 convolution_add_fusion.24
  43.3 0.9 convolution_add_fusion.23
  44.7 0.9 convolution_add_fusion.22
  45.6 0.9 convolution_add_fusion.21
  46.9 0.9 convolution_add_fusion.20
  48.2 0.9 convolution_add_fusion.19
  49.5 0.9 convolution_add_fusion.18
  50.9 2.4 convolution_add_fusion.17
  54.5 0.8 convolution_add_fusion.15
  58.0 1.3 fusion.19
  59.3 0.9 convolution_add_fusion.13
  60.6 0.9 convolution_add_fusion.12
  62.0 0.9 convolution_add_fusion.11
  63.3 2.4 convolution_add_fusion.10
  67.9 2.4 convolution_add_fusion.6
  70.3 2.5 convolution_add_fusion.5
  72.9 2.0 convolution_add_fusion.4
  74.9 2.0 convolution_add_fusion.3
  76.9 2.1 convolution_add_fusion.2
  79.9 2.0 fusion.4
  81.9 2.0 fusion.2
  84.5 1.0 copy-done.22
  88.1 4.2 %broadcast_in_dim.20 = bf16[4,1,320,3072]{3,2,1,0:T(8,128)(2,1)} broadcast(bf16[320,3072]{1,0:T(8,128)(2,1)S(1)} %multiply_convert_fusion), dimensions={2,3} | broadcast | bytes 9830400 | tf_op jit(solution)/shard_map/broadcast_in_dim | solution.py:20
  92.3 6.9 %all-to-all-start = ((bf16[4,1,320,3072]{3,2,1,0:T(8,128)(2,1)}), bf16[4,1,320,3072]{3,2,1,0:T(8,128)(2,1)}, u32[]{:S(2)}, u32[]{:S(2)}) async-start(bf16[4,1,320,3072]{3,2,1,0:T(8,128)(2,1)} %broadcast_in_dim.20), calls=%async_computation | async-start | bytes 15728640 | tf_op jit(solution)/shard_map/all_to_all | solution.py:19
  99.2 50.1 %all-gather.6.cloned.1.call-done = bf16[32,96,1152]{2,1,0:T(8,128)(2,1)} async-done(((bf16[8,96,1152]{2,1,0:T(8,128)(2,1)}), bf16[32,96,1152]{2,1,0:T(8,128)(2,1)}) %all-gather.6.cloned.1.call-update) | async-done | bytes 7077904 | tf_op jit(solution)/shard_map/all_gather | solution.py:38
  149.3 6.7 %copy.61 = bf16[2,4,4,96,1152]{4,3,2,1,0:T(8,128)(2,1)} copy(bf16[2,4,4,96,1152]{4,3,0,1,2:T(8,128)(2,1)} %bitcast.178) | data formatting | bytes 14155776 | tf_op jit(solution)/shard_map/transpose | solution.py:42
  156.1 29.8 %all-to-all-done = bf16[4,1,320,3072]{3,2,1,0:T(8,128)(2,1)} async-done(((bf16[4,1,320,3072]{3,2,1,0:T(8,128)(2,1)}), bf16[4,1,320,3072]{3,2,1,0:T(8,128)(2,1)}, u32[]{:S(2)}, u32[]{:S(2)}) %all-to-all-start) | async-done | bytes 7864352 | tf_op jit(solution)/shard_map/all_to_all | solution.py:19
  186.4 4.3 %all-to-all-start.2 = ((s32[4,1,1]{2,1,0:T(1,128)}), s32[4,1,1]{2,1,0:T(1,128)S(1)}, u32[]{:S(2)}, u32[]{:S(2)}) async-start(s32[4,1,1]{2,1,0:T(1,128)} %broadcast_in_dim.22), calls=%async_computation.2 | async-start | bytes 4096 | tf_op jit(solution)/shard_map/all_to_all | solution.py:19
  190.8 14.7 %convolution_convert_fusion = bf16[1280,1152]{1,0:T(8,128)(2,1)S(1)} fusion(bf16[1280,3072]{1,0:T(8,128)(2,1)} %bitcast.61, bf16[3072,1152]{1,0:T(8,128)(2,1)} %bitcast.179), kind=kOutput, calls=%fused_computation.25 | convolution fusion | flops 9061171200 | bytes 17891328 | tf_op jit(solution)/shard_map/dot_general | solution.py:128
  205.5 4.3 %reshape.226 = bf16[4,5,64,3,384]{4,3,2,1,0:T(4,128)(2,1)} reshape(bf16[1280,1152]{1,0:T(8,128)(2,1)S(1)} %convolution_convert_fusion) | data formatting | bytes 5898240 | tf_op jit(solution)/shard_map/reshape | solution.py:131
  209.8 7.5 %copy.62 = bf16[4,5,64,3,384]{4,0,3,1,2:T(4,128)(2,1)} copy(bf16[4,5,64,3,384]{4,3,2,1,0:T(4,128)(2,1)} %reshape.226) | data formatting | bytes 5898240 | tf_op jit(solution)/shard_map/reshape | solution.py:131
  217.4 17.6 %all-to-all-start.1 = ((bf16[4,5,64,3,384]{4,0,3,1,2:T(4,128)(2,1)}), bf16[4,5,64,3,384]{4,0,3,1,2:T(4,128)(2,1)S(1)}, u32[]{:S(2)}, u32[]{:S(2)}) async-start(bf16[4,5,64,3,384]{4,0,3,1,2:T(4,128)(2,1)} %copy.62), calls=%async_computation.1 | async-start | bytes 5898240 | tf_op jit(solution)/shard_map/all_to_all | solution.py:134
  235.4 37.3 %all-to-all-done.1 = bf16[4,5,64,3,384]{4,0,3,1,2:T(4,128)(2,1)S(1)} async-done(((bf16[4,5,64,3,384]{4,0,3,1,2:T(4,128)(2,1)}), bf16[4,5,64,3,384]{4,0,3,1,2:T(4,128)(2,1)S(1)}, u32[]{:S(2)}, u32[]{:S(2)}) %all-to-all-start.1) | async-done | bytes 2949152 | tf_op jit(solution)/shard_map/all_to_all | solution.py:134
  272.7 2.3 copy.63
  275.0 2.1 fusion.83
  277.8 1.4 fusion.84
  279.2 1.0 fusion.17
  281.0 25.4 %all_to_all.62 = bf16[4,160,2,3,128]{4,0,3,2,1:T(4,128)(2,1)S(1)} all-to-all(bf16[4,160,2,3,128]{4,0,3,2,1:T(4,128)(2,1)S(1)} %copy.68), channel_id=1, replica_groups=mesh['dp'=4,'ctx_0'=2,'ctx_1'=4,'ctx_2'=4] {'ctx_0','ctx_1','ctx_2'}, dimensions={1} | all-to-all | bytes 1966080 | tf_op jit(solution)/shard_map/all_to_all | solution.py:70
  307.2 1.1 copy.70
  308.3 21.2 %all_to_all.63 = bf16[4,5,64,3,128]{4,2,3,1,0:T(8,128)(2,1)S(1)} all-to-all(bf16[4,5,64,3,128]{4,2,3,1,0:T(8,128)(2,1)S(1)} %bitcast.208), channel_id=1, replica_groups=mesh['dp'=4,'ctx_0'=2,'ctx_1'=4,'ctx_2'=4] {'dp'}, dimensions={0} | all-to-all | bytes 1966080 | tf_op jit(solution)/shard_map/all_to_all | solution.py:135
  329.5 0.8 copy.71
  330.3 1.6 reshape.227
  (106 shorter events, 20.3 us)
Async XLA Ops:
  7.2 79.6 %copy-start = (bf16[64,3072]{1,0:T(8,128)(2,1)S(1)}, bf16[64,3072]{1,0:T(8,128)(2,1)}, u32[]{:S(2)}) copy-start(bf16[64,3072]{1,0:T(8,128)(2,1)} %param.13) | copy-start | bytes 1179652
  7.2 6.7 %copy-start.28 = (bf16[96,1152]{1,0:T(8,128)(2,1)S(1)}, bf16[96,1152]{1,0:T(8,128)(2,1)}, u32[]{:S(2)}) copy-start(bf16[96,1152]{1,0:T(8,128)(2,1)} %param.15) | copy-start | bytes 663556
  7.2 60.6 %all-gather.4.cloned.1.call-start = ((), (), s32[]{:S(2)}) async-start(), calls=%async_computation.5 | async-start | bytes 2211840 | tf_op jit(solution)/shard_map/all_gather | solution.py:38
  9.5 15.0 %collective-permute-start = (bf16[1,2,16,16,512]{4,3,2,1,0:T(8,128)(2,1)S(1)}, bf16[1,2,16,16,512]{4,3,2,1,0:T(8,128)(2,1)S(1)}, u32[]{:S(2)}, u32[]{:S(2)}) collective-permute-start(bf16[1,2,16,16,512]{4,3,2,1,0:T(8,128)(2,1)S(1)} %slice.235), channel_id=1, source_target_pairs={{0,1},{1,2},{2,3},{3,4},{4,5},{5,6},{6,7},{7,8},{8,9},{9,10},{10,1... | collective-permute-start | bytes 1572872 | tf_op jit(solution)/shard_map/ppermute | solution.py:14
  22.2 127.1 %all-gather.6.cloned.1.call-start = ((), (), s32[]{:S(2)}) async-start(), calls=%async_computation.6 | async-start | bytes 8847360 | tf_op jit(solution)/shard_map/all_gather | solution.py:38
  24.4 15.2 %slice-start = ((s8[14155776]{0:T(1024)(128)(4,1)}), s8[4194304]{0:T(1024)(128)(4,1)S(1)}, s32[]{:S(2)}) async-start(s8[14155776]{0:T(1024)(128)(4,1)} %bitcast.173), calls=%async_computation.7 | async-start | bytes 8388608
  24.6 15.1 %slice-start.1 = ((s8[14155776]{0:T(1024)(128)(4,1)}), s8[4194304]{0:T(1024)(128)(4,1)S(1)}, s32[]{:S(2)}) async-start(s8[14155776]{0:T(1024)(128)(4,1)} %bitcast.173), calls=%async_computation.8 | async-start | bytes 8388608
  24.6 15.0 %slice-start.2 = ((s8[14155776]{0:T(1024)(128)(4,1)}), s8[4194304]{0:T(1024)(128)(4,1)S(1)}, s32[]{:S(2)}) async-start(s8[14155776]{0:T(1024)(128)(4,1)} %bitcast.173), calls=%async_computation.9 | async-start | bytes 8388608
  24.6 15.0 %slice-start.3 = ((s8[14155776]{0:T(1024)(128)(4,1)}), s8[1572864]{0:T(1024)(128)(4,1)S(1)}, s32[]{:S(2)}) async-start(s8[14155776]{0:T(1024)(128)(4,1)} %bitcast.173), calls=%async_computation.10 | async-start | bytes 3145728
  40.5 1.4 copy-start.17
  41.9 1.4 copy-start.16
  43.3 1.4 copy-start.15
  45.6 1.3 copy-start.14
  46.9 1.3 copy-start.13
  48.2 1.3 copy-start.12
  49.5 1.3 copy-start.11
  50.9 2.4 copy-start.10
  53.2 1.3 copy-start.9
  54.5 1.3 copy-start.8
  55.8 1.3 copy-start.18
  59.3 1.3 copy-start.7
  60.6 1.3 copy-start.6
  62.0 1.3 copy-start.5
  65.6 1.3 copy-start.4
  67.9 2.4 copy-start.23
  70.3 2.5 copy-start.26
  72.9 2.0 copy-start.25
  74.9 2.0 copy-start.24
  76.9 2.1 copy-start.2
  76.9 2.7 copy-start.3
  76.9 3.0 copy-start.20
  79.9 2.0 copy-start.19
  81.9 2.0 copy-start.21
  84.0 1.6 copy-start.29
  84.5 1.1 copy-start.22
  84.5 2.2 copy-start.27
  86.7 0.8 copy-start.30
  92.3 93.5 %all-to-all-start = ((bf16[4,1,320,3072]{3,2,1,0:T(8,128)(2,1)}), bf16[4,1,320,3072]{3,2,1,0:T(8,128)(2,1)}, u32[]{:S(2)}, u32[]{:S(2)}) async-start(bf16[4,1,320,3072]{3,2,1,0:T(8,128)(2,1)} %broadcast_in_dim.20), calls=%async_computation | async-start | bytes 15728640 | tf_op jit(solution)/shard_map/all_to_all | solution.py:19
  186.4 30.9 %all-to-all-start.2 = ((s32[4,1,1]{2,1,0:T(1,128)}), s32[4,1,1]{2,1,0:T(1,128)S(1)}, u32[]{:S(2)}, u32[]{:S(2)}) async-start(s32[4,1,1]{2,1,0:T(1,128)} %broadcast_in_dim.22), calls=%async_computation.2 | async-start | bytes 4096 | tf_op jit(solution)/shard_map/all_to_all | solution.py:19
  217.4 55.4 %all-to-all-start.1 = ((bf16[4,5,64,3,384]{4,0,3,1,2:T(4,128)(2,1)}), bf16[4,5,64,3,384]{4,0,3,1,2:T(4,128)(2,1)S(1)}, u32[]{:S(2)}, u32[]{:S(2)}) async-start(bf16[4,5,64,3,384]{4,0,3,1,2:T(4,128)(2,1)} %copy.62), calls=%async_computation.1 | async-start | bytes 5898240 | tf_op jit(solution)/shard_map/all_to_all | solution.py:134
  308.3 23.7 %copy-start.1 = (bf16[64,3072]{1,0:T(8,128)(2,1)S(1)}, bf16[64,3072]{1,0:T(8,128)(2,1)}, u32[]{:S(2)}) copy-start(bf16[64,3072]{1,0:T(8,128)(2,1)} %param.13) | copy-start | bytes 1179652
Sparse Core Ops, SparseCore 0:
  22.3 38.4 all-gather.3
  68.0 81.3 all-gather.5
where the time goes:
time: 344 us; the launch traced here: 339 us
  waiting for transfers between devices  119 us (35%)
  local copies, waits for them, and re-layouts  57.4 us (17%)
  blocking collectives  54.9 us (16%)
  matrix products  52.6 us (15%)
  starting transfers between devices  33.3 us (10%)
  between operations  15.6 us (5%)
  other arithmetic  6.67 us (2%)
    all_gather x2, waiting for transfers between devices, all_blocks(): tiles = lax.all_gather(tiles, axes[k], axis=0, tiled=True)  50.1 us
    all_to_all x1, waiting for transfers between devices, on_device(): lax.all_to_all(qkv, CTX, split_axis=2, concat_axis=1, tiled=True)  37.3 us
    dot_general x27, matrix products, on_device(): jnp.dot(slab, conv_weight[lag, row, col], preferred_element_type=jnp.floa...  35 us
    all_to_all x2, waiting for transfers between devices, from_everyone(): lax.all_to_all(jnp.broadcast_to(array[None], (length, *array.shape)), axi...  29.8 us
    all_to_all x1, blocking collectives, attend(): return lax.all_to_all(out, CTX, split_axis=1, concat_axis=2, tiled=True)  25.4 us
    all_to_all x1, blocking collectives, on_device(): mixed = lax.all_to_all(mixed, 'dp', split_axis=0, concat_axis=3, tiled=True)  21.2 us
    all_to_all x1, starting transfers between devices, on_device(): lax.all_to_all(qkv, CTX, split_axis=2, concat_axis=1, tiled=True)  17.6 us
    slice x2, local copies, waits for them, and re-layouts, on_device(): padded[2 - lag:2 - lag + f_dev, row:row + height, col:col + width, :]  15 us
  transfers between devices with their start and end apart: 6, of which 4 were waited for; matrix products, arithmetic and copies ran while one was open for 27% of the time, Pallas kernels for 0%

commit v1 on v0

--- a/solution.py
+++ b/solution.py
@@ -35,7 +35,10 @@
 def all_blocks(array, axes, turns):
     tiles = array[None]
     for k in turns:
-        tiles = lax.all_gather(tiles, axes[k], axis=0, tiled=True)
+        size = lax.axis_size(axes[k])
+        parts = jnp.stack([tiles for _ in range(size)])
+        parts = lax.all_to_all(parts, axes[k], split_axis=0, concat_axis=0)
+        tiles = jnp.concatenate(parts, axis=0)
     current = [lax.axis_size(axes[k]) for k in reversed(turns)]
     tiles = tiles.reshape(*current, *array.shape)
     turned = sorted(range(len(turns)), key=lambda place: turns[len(turns) - 1 - place])

time: 344 us -> 400 us (1.16)
  waiting for transfers between devices: 119 us -> 180 us
  between operations: 15.6 us -> 2.21 us
  starting transfers between devices: 33.3 us -> 43 us
  blocking collectives: 54.9 us -> 46.6 us
  local copies, waits for them, and re-layouts: 57.4 us -> 62.1 us
    all_to_all x0 -> x3, waiting for transfers between devices: none -> 62.7 us  [all_blocks(): parts = lax.all_to_all(parts, axes[k], split_axis=0, concat_axis=0)]
    all_gather x2 -> x0, waiting for transfers between devices: 50.1 us -> none  [all_blocks(): tiles = lax.all_gather(tiles, axes[k], axis=0, tiled=True)]
    all_to_all x2, waiting for transfers between devices: 29.8 us -> 79.9 us  [from_everyone(): lax.all_to_all(jnp.broadcast_to(array[None], (length, *array.shape)), axi...]
    all_to_all x0 -> x3, starting transfers between devices: none -> 16.1 us  [all_blocks(): parts = lax.all_to_all(parts, axes[k], split_axis=0, concat_axis=0)]
    all_to_all x1, starting transfers between devices: 17.6 us -> 8.63 us  [on_device(): lax.all_to_all(qkv, CTX, split_axis=2, concat_axis=1, tiled=True)]
    all_gather x1 -> x0, blocking collectives: 8.3 us -> none  [all_blocks(): tiles = lax.all_gather(tiles, axes[k], axis=0, tiled=True)]
    another operation x0 -> x2, local copies, waits for them, and re-layouts: none -> 6.29 us  [all_blocks(): parts = jnp.stack([tiles for _ in range(size)])]
  transfers between devices with their start and end apart: 6 -> 7, of which waited for: 4 -> 4; matrix products, arithmetic and copies ran while one was open for 27% -> 23% of each run, Pallas kernels for 0% -> 0%
where the time goes in v1:
time: 400 us; the launch traced here: 395 us
  waiting for transfers between devices  180 us (45%)
  local copies, waits for them, and re-layouts  62.1 us (16%)
  matrix products  53.3 us (13%)
  blocking collectives  46.6 us (12%)
  starting transfers between devices  43 us (11%)
  other arithmetic  7.47 us (2%)
    all_to_all x2, waiting for transfers between devices, from_everyone(): lax.all_to_all(jnp.broadcast_to(array[None], (length, *array.shape)), axi...  79.9 us
    all_to_all x3, waiting for transfers between devices, all_blocks(): parts = lax.all_to_all(parts, axes[k], split_axis=0, concat_axis=0)  62.7 us
    all_to_all x1, waiting for transfers between devices, on_device(): lax.all_to_all(qkv, CTX, split_axis=2, concat_axis=1, tiled=True)  37.4 us
    dot_general x27, matrix products, on_device(): jnp.dot(slab, conv_weight[lag, row, col], preferred_element_type=jnp.floa...  35.7 us
    all_to_all x1, blocking collectives, attend(): return lax.all_to_all(out, CTX, split_axis=1, concat_axis=2, tiled=True)  25.2 us
    all_to_all x1, blocking collectives, on_device(): mixed = lax.all_to_all(mixed, 'dp', split_axis=0, concat_axis=3, tiled=True)  21.4 us
    all_to_all x3, starting transfers between devices, all_blocks(): parts = lax.all_to_all(parts, axes[k], split_axis=0, concat_axis=0)  16.1 us
    slice x2, local copies, waits for them, and re-layouts, on_device(): padded[2 - lag:2 - lag + f_dev, row:row + height, col:col + width, :]  15.1 us
  transfers between devices with their start and end apart: 7, of which 4 were waited for; matrix products, arithmetic and copies ran while one was open for 23% of the time, Pallas kernels for 0%

profile of v1, /device:TPU:1, one launch (start us, length us, event | category | flops | bytes accessed | tf_op | source)
XLA Modules:
  0.0 394.7 jit_solution(13035748913887990502)
XLA Ops:
  0.7 2.2 fusion.9
  2.9 4.4 %collective-permute-start = (bf16[1,2,16,16,512]{4,3,2,1,0:T(8,128)(2,1)S(1)}, bf16[1,2,16,16,512]{4,3,2,1,0:T(8,128)(2,1)S(1)}, u32[]{:S(2)}, u32[]{:S(2)}) collective-permute-start(bf16[1,2,16,16,512]{4,3,2,1,0:T(8,128)(2,1)S(1)} %slice.235), channel_id=1, source_target_pairs={{0,1},{1,2},{2,3},{3,4},{4,5},{5,6},{6,7},{7,8},{8,9},{9,10},{10,1... | collective-permute-start | bytes 1572872 | tf_op jit(solution)/shard_map/ppermute | solution.py:14
  8.1 4.0 %all-to-all-start.1 = ((bf16[2,1,96,1152]{3,2,1,0:T(8,128)(2,1)}), bf16[2,1,96,1152]{3,2,1,0:T(8,128)(2,1)S(1)}, u32[]{:S(2)}, u32[]{:S(2)}) async-start(bf16[2,1,96,1152]{3,2,1,0:T(8,128)(2,1)} %pad_maximum_fusion.1), calls=%async_computation.1 | async-start | bytes 884736 | tf_op jit(solution)/shard_map/all_to_all | solution.py:40
  12.9 6.6 %all-to-all-done.1 = bf16[2,1,96,1152]{3,2,1,0:T(8,128)(2,1)S(1)} async-done(((bf16[2,1,96,1152]{3,2,1,0:T(8,128)(2,1)}), bf16[2,1,96,1152]{3,2,1,0:T(8,128)(2,1)S(1)}, u32[]{:S(2)}, u32[]{:S(2)}) %all-to-all-start.1) | async-done | bytes 442400 | tf_op jit(solution)/shard_map/all_to_all | solution.py:40
  19.5 1.4 stack.10
  20.9 4.4 %all-to-all-start.2 = ((bf16[4,2,96,1152]{3,2,1,0:T(8,128)(2,1)}), bf16[4,2,96,1152]{3,2,1,0:T(8,128)(2,1)}, u32[]{:S(2)}, u32[]{:S(2)}) async-start(bf16[4,2,96,1152]{3,2,1,0:T(8,128)(2,1)} %stack.10), calls=%async_computation.2 | async-start | bytes 3538944 | tf_op jit(solution)/shard_map/all_to_all | solution.py:40
  25.6 11.3 %pad_slice_fusion = (bf16[5,16,16,512]{3,2,1,0:T(8,128)(2,1)}, bf16[5,16,16,512]{3,2,1,0:T(8,128)(2,1)}, bf16[5,16,16,512]{3,2,1,0:T(8,128)(2,1)}, bf16[5,16,16,...) fusion(bf16[7,16,16,512]{3,2,1,0:T(8,128)(2,1)S(1)} %fusion.15), kind=kLoop, calls=%fused_computation.1 | loop fusion | bytes 26738688 | tf_op jit(solution)/shard_map/slice | solution.py:99
  36.8 3.8 pad_slice_fusion.1
  42.8 0.9 convolution_add_fusion.24
  49.0 0.9 convolution_add_fusion.19
  50.3 0.9 convolution_add_fusion.18
  51.6 2.4 convolution_add_fusion.17
  54.0 0.9 convolution_add_fusion.16
  56.7 0.9 convolution_add_fusion.14
  57.5 1.3 fusion.19
  58.8 0.9 convolution_add_fusion.13
  63.3 2.4 convolution_add_fusion.10
  65.6 0.9 convolution_add_fusion.8
  66.5 4.9 %stack.11 = bf16[4,8,96,1152]{3,2,1,0:T(8,128)(2,1)} broadcast(bf16[8,96,1152]{2,1,0:T(8,128)(2,1)} %bitcast.64), dimensions={1,2,3} | broadcast | bytes 8847360 | tf_op jit(solution)/shard_map/stack | solution.py:39
  71.4 7.7 %all-to-all-start.3 = ((bf16[4,8,96,1152]{3,2,1,0:T(8,128)(2,1)}), bf16[4,8,96,1152]{3,2,1,0:T(8,128)(2,1)}, u32[]{:S(2)}, u32[]{:S(2)}) async-start(bf16[4,8,96,1152]{3,2,1,0:T(8,128)(2,1)} %stack.11), calls=%async_computation.3 | async-start | bytes 14155776 | tf_op jit(solution)/shard_map/all_to_all | solution.py:40
  79.1 2.4 convolution_add_fusion.7
  81.6 2.0 convolution_add_fusion.6
  83.6 2.0 convolution_add_fusion.5
  85.6 2.0 convolution_add_fusion.4
  87.6 2.0 convolution_add_fusion.3
  89.6 2.1 convolution_add_fusion.2
  92.7 2.0 fusion.4
  94.7 2.0 fusion.2
  97.3 1.0 copy-done.21
  100.9 56.0 %all-to-all-done.3 = bf16[4,8,96,1152]{3,2,1,0:T(8,128)(2,1)} async-done(((bf16[4,8,96,1152]{3,2,1,0:T(8,128)(2,1)}), bf16[4,8,96,1152]{3,2,1,0:T(8,128)(2,1)}, u32[]{:S(2)}, u32[]{:S(2)}) %all-to-all-start.3) | async-done | bytes 7077920 | tf_op jit(solution)/shard_map/all_to_all | solution.py:40
  157.0 4.1 %broadcast_in_dim.18 = bf16[4,1,320,3072]{3,2,1,0:T(8,128)(2,1)} broadcast(bf16[320,3072]{1,0:T(8,128)(2,1)S(1)} %multiply_convert_fusion), dimensions={2,3} | broadcast | bytes 9830400 | tf_op jit(solution)/shard_map/broadcast_in_dim | solution.py:20
  161.0 9.6 %all-to-all-start = ((bf16[4,1,320,3072]{3,2,1,0:T(8,128)(2,1)}), bf16[4,1,320,3072]{3,2,1,0:T(8,128)(2,1)}, u32[]{:S(2)}, u32[]{:S(2)}) async-start(bf16[4,1,320,3072]{3,2,1,0:T(8,128)(2,1)} %broadcast_in_dim.18), calls=%async_computation | async-start | bytes 15728640 | tf_op jit(solution)/shard_map/all_to_all | solution.py:19
  170.6 6.7 %copy.61 = bf16[2,4,4,96,1152]{4,3,2,1,0:T(8,128)(2,1)} copy(bf16[2,4,4,96,1152]{4,3,0,1,2:T(8,128)(2,1)} %bitcast.66) | data formatting | bytes 14155776 | tf_op jit(solution)/shard_map/transpose | solution.py:45
  177.4 79.9 %all-to-all-done = bf16[4,1,320,3072]{3,2,1,0:T(8,128)(2,1)} async-done(((bf16[4,1,320,3072]{3,2,1,0:T(8,128)(2,1)}), bf16[4,1,320,3072]{3,2,1,0:T(8,128)(2,1)}, u32[]{:S(2)}, u32[]{:S(2)}) %all-to-all-start) | async-done | bytes 7864352 | tf_op jit(solution)/shard_map/all_to_all | solution.py:19
  257.8 4.3 %all-to-all-start.5 = ((s32[4,1,1]{2,1,0:T(1,128)}), s32[4,1,1]{2,1,0:T(1,128)S(1)}, u32[]{:S(2)}, u32[]{:S(2)}) async-start(s32[4,1,1]{2,1,0:T(1,128)} %broadcast_in_dim.19), calls=%async_computation.5 | async-start | bytes 4096 | tf_op jit(solution)/shard_map/all_to_all | solution.py:19
  262.2 14.7 %convolution_convert_fusion = bf16[1280,1152]{1,0:T(8,128)(2,1)S(1)} fusion(bf16[1280,3072]{1,0:T(8,128)(2,1)} %bitcast.61, bf16[3072,1152]{1,0:T(8,128)(2,1)} %bitcast.180), kind=kOutput, calls=%fused_computation.25 | convolution fusion | flops 9061171200 | bytes 17891328 | tf_op jit(solution)/shard_map/dot_general | solution.py:131
  276.9 4.3 %reshape.226 = bf16[4,5,64,3,384]{4,3,2,1,0:T(4,128)(2,1)} reshape(bf16[1280,1152]{1,0:T(8,128)(2,1)S(1)} %convolution_convert_fusion) | data formatting | bytes 5898240 | tf_op jit(solution)/shard_map/reshape | solution.py:134
  281.2 7.5 %copy.62 = bf16[4,5,64,3,384]{4,0,3,1,2:T(4,128)(2,1)} copy(bf16[4,5,64,3,384]{4,3,2,1,0:T(4,128)(2,1)} %reshape.226) | data formatting | bytes 5898240 | tf_op jit(solution)/shard_map/reshape | solution.py:134
  288.8 8.6 %all-to-all-start.4 = ((bf16[4,5,64,3,384]{4,0,3,1,2:T(4,128)(2,1)}), bf16[4,5,64,3,384]{4,0,3,1,2:T(4,128)(2,1)S(1)}, u32[]{:S(2)}, u32[]{:S(2)}) async-start(bf16[4,5,64,3,384]{4,0,3,1,2:T(4,128)(2,1)} %copy.62), calls=%async_computation.4 | async-start | bytes 5898240 | tf_op jit(solution)/shard_map/all_to_all | solution.py:137
  297.9 37.4 %all-to-all-done.4 = bf16[4,5,64,3,384]{4,0,3,1,2:T(4,128)(2,1)S(1)} async-done(((bf16[4,5,64,3,384]{4,0,3,1,2:T(4,128)(2,1)}), bf16[4,5,64,3,384]{4,0,3,1,2:T(4,128)(2,1)S(1)}, u32[]{:S(2)}, u32[]{:S(2)}) %all-to-all-start.4) | async-done | bytes 2949152 | tf_op jit(solution)/shard_map/all_to_all | solution.py:137
  335.2 2.3 copy.63
  337.5 2.1 fusion.83
  340.3 1.4 fusion.84
  341.7 1.0 fusion.17
  343.5 25.2 %all_to_all.77 = bf16[4,160,2,3,128]{4,0,3,2,1:T(4,128)(2,1)S(1)} all-to-all(bf16[4,160,2,3,128]{4,0,3,2,1:T(4,128)(2,1)S(1)} %copy.68), channel_id=1, replica_groups=mesh['dp'=4,'ctx_0'=2,'ctx_1'=4,'ctx_2'=4] {'ctx_0','ctx_1','ctx_2'}, dimensions={1} | all-to-all | bytes 1966080 | tf_op jit(solution)/shard_map/all_to_all | solution.py:73
  369.5 1.1 copy.70
  370.6 21.4 %all_to_all.78 = bf16[4,5,64,3,128]{4,2,3,1,0:T(8,128)(2,1)S(1)} all-to-all(bf16[4,5,64,3,128]{4,2,3,1,0:T(8,128)(2,1)S(1)} %bitcast.209), channel_id=1, replica_groups=mesh['dp'=4,'ctx_0'=2,'ctx_1'=4,'ctx_2'=4] {'dp'}, dimensions={0} | all-to-all | bytes 1966080 | tf_op jit(solution)/shard_map/all_to_all | solution.py:138
  392.8 1.6 reshape.227
  (108 shorter events, 22.9 us)
Async XLA Ops:
  0.6 98.9 %copy-start = (bf16[64,3072]{1,0:T(8,128)(2,1)S(1)}, bf16[64,3072]{1,0:T(8,128)(2,1)}, u32[]{:S(2)}) copy-start(bf16[64,3072]{1,0:T(8,128)(2,1)} %param.13) | copy-start | bytes 1179652
  0.6 6.6 %copy-start.28 = (bf16[96,1152]{1,0:T(8,128)(2,1)S(1)}, bf16[96,1152]{1,0:T(8,128)(2,1)}, u32[]{:S(2)}) copy-start(bf16[96,1152]{1,0:T(8,128)(2,1)} %param.15) | copy-start | bytes 663556
  2.9 22.5 %collective-permute-start = (bf16[1,2,16,16,512]{4,3,2,1,0:T(8,128)(2,1)S(1)}, bf16[1,2,16,16,512]{4,3,2,1,0:T(8,128)(2,1)S(1)}, u32[]{:S(2)}, u32[]{:S(2)}) collective-permute-start(bf16[1,2,16,16,512]{4,3,2,1,0:T(8,128)(2,1)S(1)} %slice.235), channel_id=1, source_target_pairs={{0,1},{1,2},{2,3},{3,4},{4,5},{5,6},{6,7},{7,8},{8,9},{9,10},{10,1... | collective-permute-start | bytes 1572872 | tf_op jit(solution)/shard_map/ppermute | solution.py:14
  8.1 11.4 %all-to-all-start.1 = ((bf16[2,1,96,1152]{3,2,1,0:T(8,128)(2,1)}), bf16[2,1,96,1152]{3,2,1,0:T(8,128)(2,1)S(1)}, u32[]{:S(2)}, u32[]{:S(2)}) async-start(bf16[2,1,96,1152]{3,2,1,0:T(8,128)(2,1)} %pad_maximum_fusion.1), calls=%async_computation.1 | async-start | bytes 884736 | tf_op jit(solution)/shard_map/all_to_all | solution.py:40
  20.9 45.6 %all-to-all-start.2 = ((bf16[4,2,96,1152]{3,2,1,0:T(8,128)(2,1)}), bf16[4,2,96,1152]{3,2,1,0:T(8,128)(2,1)}, u32[]{:S(2)}, u32[]{:S(2)}) async-start(bf16[4,2,96,1152]{3,2,1,0:T(8,128)(2,1)} %stack.10), calls=%async_computation.2 | async-start | bytes 3538944 | tf_op jit(solution)/shard_map/all_to_all | solution.py:40
  25.3 15.3 %slice-start = ((s8[14155776]{0:T(1024)(128)(4,1)}), s8[4194304]{0:T(1024)(128)(4,1)S(1)}, s32[]{:S(2)}) async-start(s8[14155776]{0:T(1024)(128)(4,1)} %bitcast.175), calls=%async_computation.8 | async-start | bytes 8388608
  25.5 15.1 %slice-start.1 = ((s8[14155776]{0:T(1024)(128)(4,1)}), s8[4194304]{0:T(1024)(128)(4,1)S(1)}, s32[]{:S(2)}) async-start(s8[14155776]{0:T(1024)(128)(4,1)} %bitcast.175), calls=%async_computation.9 | async-start | bytes 8388608
  25.5 15.1 %slice-start.2 = ((s8[14155776]{0:T(1024)(128)(4,1)}), s8[4194304]{0:T(1024)(128)(4,1)S(1)}, s32[]{:S(2)}) async-start(s8[14155776]{0:T(1024)(128)(4,1)} %bitcast.175), calls=%async_computation.10 | async-start | bytes 8388608
  25.5 15.1 %slice-start.3 = ((s8[14155776]{0:T(1024)(128)(4,1)}), s8[1572864]{0:T(1024)(128)(4,1)S(1)}, s32[]{:S(2)}) async-start(s8[14155776]{0:T(1024)(128)(4,1)} %bitcast.175), calls=%async_computation.11 | async-start | bytes 3145728
  41.5 1.3 copy-start.16
  42.8 1.3 copy-start.15
  44.1 1.3 copy-start.14
  46.3 1.3 copy-start.13
  47.6 1.3 copy-start.12
  49.0 1.3 copy-start.11
  50.3 1.3 copy-start.10
  51.6 2.4 copy-start.9
  54.0 1.3 copy-start.8
  55.3 1.3 copy-start.7
  58.8 1.3 copy-start.6
  60.1 1.3 copy-start.17
  61.0 1.4 copy-start.5
  63.3 2.4 copy-start.4
  71.4 85.5 %all-to-all-start.3 = ((bf16[4,8,96,1152]{3,2,1,0:T(8,128)(2,1)}), bf16[4,8,96,1152]{3,2,1,0:T(8,128)(2,1)}, u32[]{:S(2)}, u32[]{:S(2)}) async-start(bf16[4,8,96,1152]{3,2,1,0:T(8,128)(2,1)} %stack.11), calls=%async_computation.3 | async-start | bytes 14155776 | tf_op jit(solution)/shard_map/all_to_all | solution.py:40
  79.1 2.4 copy-start.26
  81.6 2.0 copy-start.22
  83.6 2.0 copy-start.25
  85.6 2.0 copy-start.24
  87.6 2.0 copy-start.23
  89.6 2.1 copy-start.2
  89.6 2.7 copy-start.3
  89.6 3.0 copy-start.19
  92.7 2.0 copy-start.18
  94.7 2.0 copy-start.20
  96.7 1.7 copy-start.29
  97.3 1.1 copy-start.21
  97.3 2.2 copy-start.27
  99.5 0.8 copy-start.30
  161.0 96.2 %all-to-all-start = ((bf16[4,1,320,3072]{3,2,1,0:T(8,128)(2,1)}), bf16[4,1,320,3072]{3,2,1,0:T(8,128)(2,1)}, u32[]{:S(2)}, u32[]{:S(2)}) async-start(bf16[4,1,320,3072]{3,2,1,0:T(8,128)(2,1)} %broadcast_in_dim.18), calls=%async_computation | async-start | bytes 15728640 | tf_op jit(solution)/shard_map/all_to_all | solution.py:19
  257.8 30.9 %all-to-all-start.5 = ((s32[4,1,1]{2,1,0:T(1,128)}), s32[4,1,1]{2,1,0:T(1,128)S(1)}, u32[]{:S(2)}, u32[]{:S(2)}) async-start(s32[4,1,1]{2,1,0:T(1,128)} %broadcast_in_dim.19), calls=%async_computation.5 | async-start | bytes 4096 | tf_op jit(solution)/shard_map/all_to_all | solution.py:19
  288.8 46.4 %all-to-all-start.4 = ((bf16[4,5,64,3,384]{4,0,3,1,2:T(4,128)(2,1)}), bf16[4,5,64,3,384]{4,0,3,1,2:T(4,128)(2,1)S(1)}, u32[]{:S(2)}, u32[]{:S(2)}) async-start(bf16[4,5,64,3,384]{4,0,3,1,2:T(4,128)(2,1)} %copy.62), calls=%async_computation.4 | async-start | bytes 5898240 | tf_op jit(solution)/shard_map/all_to_all | solution.py:137
  370.6 23.9 %copy-start.1 = (bf16[64,3072]{1,0:T(8,128)(2,1)S(1)}, bf16[64,3072]{1,0:T(8,128)(2,1)}, u32[]{:S(2)}) copy-start(bf16[64,3072]{1,0:T(8,128)(2,1)} %param.13) | copy-start | bytes 1179652
